TPU v7x, 512 devices: a whole 4x8x8 slice. The times are simulated.
512 devices in a mesh: energy: 32 (over y_lo, z, core), slab: 16 (over x, y_hi).
Axes of the slice: x: 4, y: 8 (y_hi: 4, y_lo: 2; y = y_hi * 2 + y_lo), z: 8, core: 2. Of those that a mesh axis runs over, the one named last changes fastest.
Arguments:
- green_old: bfloat16 [64, 16, 2, 256, 256], P('energy', 'slab'), may hold values from -1.25 to 1.25
- hopping: bfloat16 [16, 256, 256], P('slab'), may hold values from -0.0390625 to 0.0390625
- phonon_coupling: bfloat16 [16, 3, 256, 256], P('slab'), may hold values from -0.03125 to 0.03125
- band_offset: float32 [16, 256], P('slab'), may hold values from 0.35 to 0.55
- interface: float32 [16, 64, 64], P('slab'), may hold values from -0.09375 to 0.09375
- cell_counts: int32 [16], P('slab'), may hold values from 1 to 8, 80 in all
- contact_flags: int32 [16], P('slab'), may hold values 0 or 1
- phonon_shift: int32 [3], replicated, may hold values from 1 to 6, as said below
Outputs:
- green_new: float32 [64, 16, 2, 256, 256], P('energy', 'slab')
Inputs may be any that keep to these rules, and one draw needn't show every extreme that they name: `phonon_shift`: mode k, counted from 0, has an offset from k * 2 + 1 to (k + 1) * 2; the last mode takes its top value.
All inputs are finite; a program needn't handle non-finite values. No bound on the sum of `cell_counts` or of `contact_flags` on one device may be relied on, other than what follows from the above.
Results may differ from a plain program's by a relative error of at most 0.0023.
Values may be sent and summed in bfloat16 or wider, within the bound.
No kernel may reach another device: no remote copies, remote signals or barrier semaphores. Data moves between devices by JAX's collectives and lax.ppermute only.
A program may use at most 64 MiB of HBM per device.

v0:
```python
import jax
import jax.numpy as jnp
from jax import lax
from jax.sharding import PartitionSpec as P

MODES = 3
NS_STEPS = 3
MAXCELL = 8


broadening = 0.05
contact_width = 0.15
damping = 0.75
level_start = -0.05
level_range = 0.1
highest = lax.Precision.HIGHEST


def from_behind(value, axis, steps):
    count = lax.axis_size(axis)
    first, last = (max(0, -steps), min(count, count - steps))
    return lax.ppermute(value, axis, [(source, source + steps) for source in range(first, last)])


def from_behind_2(value, axis, steps):
    count = lax.axis_size(axis)
    pairs = [(source, (source + steps) % count) for source in range(count)]
    return lax.ppermute(value, axis, pairs)


def complex_product(left, right):
    real_real = jnp.einsum("xij,xjk->xik", left[:, 0], right[:, 0], precision=highest)
    imag_imag = jnp.einsum("xij,xjk->xik", left[:, 1], right[:, 1], precision=highest)
    real_imag = jnp.einsum("xij,xjk->xik", left[:, 0], right[:, 1], precision=highest)
    imag_real = jnp.einsum("xij,xjk->xik", left[:, 1], right[:, 0], precision=highest)
    return jnp.stack((real_real - imag_imag, real_imag + imag_real), 1)


def scale_columns(matrix, diagonal):
    real_col = diagonal[:, 0, None, :]
    imag_col = diagonal[:, 1, None, :]
    real_part = matrix[:, 0] * real_col - matrix[:, 1] * imag_col
    imag_part = matrix[:, 0] * imag_col + matrix[:, 1] * real_col
    return jnp.stack((real_part, imag_part), 1)


def scale_rows(matrix, diagonal):
    real_row = diagonal[:, 0, :, None]
    imag_row = diagonal[:, 1, :, None]
    real_part = real_row * matrix[:, 0] - imag_row * matrix[:, 1]
    imag_part = real_row * matrix[:, 1] + imag_row * matrix[:, 0]
    return jnp.stack((real_part, imag_part), 1)


def pass_faces(left_face, right_face):
    from_left = from_behind(right_face, "slab", 1)
    from_right = from_behind(left_face, "slab", -1)
    return (from_left, from_right)


def on_device(
    green_old,
    hopping,
    phonon_coupling,
    band_offset,
    interface,
    cell_counts,
    contact_flags,
    phonon_shift,
):
    per_device = green_old.shape[0]
    orbitals = green_old.shape[3]
    face = interface.shape[1]
    energies = per_device * lax.axis_size("energy")
    own_block = green_old[:, 0]
    nearby = {0: own_block}
    going_down = own_block
    going_up = own_block
    for stop_index in range(1, MODES + 1):
        going_down = from_behind_2(going_down, "energy", 1)
        going_up = from_behind_2(going_up, "energy", -1)
        nearby[-stop_index] = going_down
        nearby[stop_index] = going_up
    local_index = jnp.arange(per_device, dtype=jnp.int32)
    weight = cell_counts[0].astype(jnp.float32) / MAXCELL
    total = jnp.zeros(own_block.shape, jnp.float32)
    for mode in range(MODES):
        shift_count = phonon_shift[mode]
        pair = jnp.zeros(own_block.shape, jnp.float32)
        for direction, candidates in ((-1, (-(mode + 1), -mode)), (1, (mode, mode + 1))):
            target = local_index + direction * shift_count
            offset = jnp.floor_divide(target, per_device)
            within = target - offset * per_device
            for place in candidates:
                picked = jnp.take(nearby[place], within, axis=0).astype(jnp.float32)
                pair = pair + jnp.where((offset == place)[:, None, None, None], picked, 0.0)
        pair = pair.astype(jnp.bfloat16)
        matrix = phonon_coupling[0, mode]
        half = jnp.einsum("ij,xcjl->xcil", matrix, pair, preferred_element_type=jnp.float32).astype(
            jnp.bfloat16
        )
        total = total + jnp.einsum(
            "xcil,ml->xcim", half, matrix, preferred_element_type=jnp.float32
        )
    sigma = total * weight
    energy_index = lax.axis_index("energy") * per_device + local_index
    level = level_start + level_range * energy_index.astype(jnp.float32) / energies
    real_diag = level[:, None] + band_offset[0][None, :]
    width = broadening + contact_width * contact_flags[0].astype(jnp.float32)
    imag_diag = jnp.broadcast_to(width, real_diag.shape)
    eye_big = jnp.eye(orbitals, dtype=jnp.float32)
    eye_face = jnp.eye(face, dtype=jnp.float32)
    symmetric = 0.5 * (hopping[0].astype(jnp.float32) + hopping[0].T.astype(jnp.float32))
    base = (
        jnp.stack((eye_big * real_diag[:, None, :] - symmetric, eye_big * imag_diag[:, None, :]), 1)
        - sigma
    )
    denom = real_diag * real_diag + imag_diag * imag_diag
    diagonal = jnp.stack((real_diag / denom, -imag_diag / denom), 1)
    left_coupling = from_behind(interface, "slab", 1)[0]
    own_coupling = interface[0]
    iterate = eye_big * diagonal[:, :, None, :]
    for step in range(NS_STEPS):
        if step == 0:
            left_face = eye_face * diagonal[:, :, None, :face]
            right_face = eye_face * diagonal[:, :, None, orbitals - face :]
        else:
            left_face = iterate[:, :, :face, :face]
            right_face = iterate[:, :, orbitals - face :, orbitals - face :]
        from_left, from_right = pass_faces(left_face, right_face)
        inner = jnp.einsum("ba,xcbd->xcad", left_coupling, from_left, precision=highest)
        inner = jnp.einsum("xcad,de->xcae", inner, left_coupling, precision=highest)
        outer = jnp.einsum("ab,xcbd->xcad", own_coupling, from_right, precision=highest)
        outer = jnp.einsum("xcad,ed->xcae", outer, own_coupling, precision=highest)
        system = base.at[:, :, :face, :face].add(-inner)
        system = system.at[:, :, orbitals - face :, orbitals - face :].add(-outer)
        if step == 0:
            residual = -scale_columns(system, diagonal)
            residual = residual.at[:, 0].add(eye_big)
            iterate = iterate + damping * scale_rows(residual, diagonal)
        else:
            residual = -complex_product(system, iterate)
            residual = residual.at[:, 0].add(eye_big)
            iterate = iterate + damping * complex_product(iterate, residual)
    return iterate[:, None]


def solution(mesh):
    placed = (
        P("energy", "slab", None, None, None),
        P("slab", None, None),
        P("slab", None, None, None),
        P("slab", None),
        P("slab", None, None),
        P("slab"),
        P("slab"),
        P(),
    )
    return jax.shard_map(
        on_device,
        mesh=mesh,
        in_specs=placed,
        out_specs=P("energy", "slab", None, None, None),
        check_vma=False,
    )
```

profile of v0, /device:TPU:6, one launch (start us, length us, event | category | flops | bytes accessed | tf_op | source)
XLA Modules:
  0.0 148.9 jit_solution(6678229408915962506)
XLA Ops:
  0.0 11.4 %collective-permute-start.1 = (bf16[2,2,256,256]{3,2,1,0:T(8,128)(2,1)}, bf16[2,2,256,256]{3,2,1,0:T(8,128)(2,1)S(1)}, u32[]{:S(2)}, u32[]{:S(2)}) collective-permute-start(bf16[2,2,256,256]{3,2,1,0:T(8,128)(2,1)} %bitcast.226), channel_id=1, source_target_pairs={{0,496},{16,0},{32,16},{48,32},{64,48},{80,64},{96,80},{112,96},{1... | collective-permute-start | bytes 1572872 | tf_op jit(solution)/shard_map/ppermute | solution.py:28
  11.4 1.9 %collective-permute-start = (bf16[2,2,256,256]{3,2,1,0:T(8,128)(2,1)}, bf16[2,2,256,256]{3,2,1,0:T(8,128)(2,1)S(1)}, u32[]{:S(2)}, u32[]{:S(2)}) collective-permute-start(bf16[2,2,256,256]{3,2,1,0:T(8,128)(2,1)} %bitcast.227), channel_id=1, source_target_pairs={{0,16},{16,32},{32,48},{48,64},{64,80},{80,96},{96,112},{112,128},... | collective-permute-start | bytes 1572872 | tf_op jit(solution)/shard_map/ppermute | solution.py:28
  15.6 4.5 %collective-permute-start.6 = (f32[2,2,64,64]{3,2,1,0:T(8,128)}, f32[2,2,64,64]{3,2,1,0:T(8,128)}, u32[]{:S(2)}, u32[]{:S(2)}) collective-permute-start(f32[2,2,64,64]{3,2,1,0:T(8,128)} %get-tuple-element.123), channel_id=1, source_target_pairs={{0,1},{1,2},{2,3},{3,4},{4,5},{5,6},{6,7},{7,8},{8,9},{9,10},{10,1... | collective-permute-start | bytes 196616 | tf_op jit(solution)/shard_map/ppermute | solution.py:22
  20.1 4.8 %collective-permute-start.7 = (f32[1,64,64]{2,1,0:T(8,128)S(1)}, f32[1,64,64]{2,1,0:T(8,128)S(1)}, u32[]{:S(2)}, u32[]{:S(2)}) collective-permute-start(f32[1,64,64]{2,1,0:T(8,128)S(1)} %copy-done.12), channel_id=1, source_target_pairs={{0,1},{1,2},{2,3},{3,4},{4,5},{5,6},{6,7},{7,8},{8,9},{9,10},{10,1... | collective-permute-start | bytes 49160 | tf_op jit(solution)/shard_map/ppermute | solution.py:22
  24.9 4.0 %collective-permute-start.8 = (f32[2,2,64,64]{3,2,1,0:T(8,128)}, f32[2,2,64,64]{3,2,1,0:T(8,128)}, u32[]{:S(2)}, u32[]{:S(2)}) collective-permute-start(f32[2,2,64,64]{3,2,1,0:T(8,128)} %get-tuple-element.122), channel_id=1, source_target_pairs={{1,0},{2,1},{3,2},{4,3},{5,4},{6,5},{7,6},{8,7},{9,8},{10,9},{11,1... | collective-permute-start | bytes 196616 | tf_op jit(solution)/shard_map/ppermute | solution.py:22
  44.7 4.9 %collective-permute-start.3 = (bf16[2,2,256,256]{3,2,1,0:T(8,128)(2,1)S(1)}, bf16[2,2,256,256]{3,2,1,0:T(8,128)(2,1)S(1)}, u32[]{:S(2)}, u32[]{:S(2)}) collective-permute-start(bf16[2,2,256,256]{3,2,1,0:T(8,128)(2,1)S(1)} %collective-permute-done.1), channel_id=1, source_target_pairs={{0,496},{16,0},{32,16},{48,32},{64,48},{80,64},{96,80},{112,96},{1... | collective-permute-start | bytes 1572872 | tf_op jit(solution)/shard_map/ppermute | solution.py:28
  49.6 1.9 %collective-permute-start.2 = (bf16[2,2,256,256]{3,2,1,0:T(8,128)(2,1)S(1)}, bf16[2,2,256,256]{3,2,1,0:T(8,128)(2,1)S(1)}, u32[]{:S(2)}, u32[]{:S(2)}) collective-permute-start(bf16[2,2,256,256]{3,2,1,0:T(8,128)(2,1)S(1)} %collective-permute-done), channel_id=1, source_target_pairs={{0,16},{16,32},{32,48},{48,64},{64,80},{80,96},{96,112},{112,128},... | collective-permute-start | bytes 1572872 | tf_op jit(solution)/shard_map/ppermute | solution.py:28
  57.3 5.7 %collective-permute-start.5 = (bf16[2,2,256,256]{3,2,1,0:T(8,128)(2,1)S(1)}, bf16[2,2,256,256]{3,2,1,0:T(8,128)(2,1)}, u32[]{:S(2)}, u32[]{:S(2)}) collective-permute-start(bf16[2,2,256,256]{3,2,1,0:T(8,128)(2,1)S(1)} %collective-permute-done.3), channel_id=1, source_target_pairs={{0,496},{16,0},{32,16},{48,32},{64,48},{80,64},{96,80},{112,96},{1... | collective-permute-start | bytes 1572872 | tf_op jit(solution)/shard_map/ppermute | solution.py:28
  63.1 1.9 %collective-permute-start.4 = (bf16[2,2,256,256]{3,2,1,0:T(8,128)(2,1)S(1)}, bf16[2,2,256,256]{3,2,1,0:T(8,128)(2,1)}, u32[]{:S(2)}, u32[]{:S(2)}) collective-permute-start(bf16[2,2,256,256]{3,2,1,0:T(8,128)(2,1)S(1)} %collective-permute-done.2), channel_id=1, source_target_pairs={{0,16},{16,32},{32,48},{48,64},{64,80},{80,96},{96,112},{112,128},... | collective-permute-start | bytes 1572872 | tf_op jit(solution)/shard_map/ppermute | solution.py:28
  65.7 3.4 %fusion.3 = f32[2,2,256,256]{3,2,1,0:T(8,128)} fusion(bf16[2,2,256,256]{3,2,1,0:T(8,128)(2,1)} %gather_fusion.3, bf16[2,2,256,256]{3,2,1,0:T(8,128)(2,1)S(1)} %gather_fusion.2, bf16[2,2,256,256]{3,2,1,0:T(8,128)(2,1)} %gather_fusion.1, bf16[2,2,256,256]{3,2,1,0:T(8,128)(2,1)} %gather_fusion, pred[2]{0:T(512)(128)(4,1)S(1)} %copy-done.21, ...), kind=kOutput, calls=%fused_computation.20 | convolution fusion | flops 272891904 | bytes 3408904 | tf_op jit(solution)/shard_map/xcil,ml->xcim/dot_general | solution.py:102
  77.2 3.6 %convolution_add_fusion.1 = f32[2,2,256,256]{3,2,1,0:T(8,128)} fusion(f32[2,2,256,256]{3,2,1,0:T(8,128)} %fusion.3, bf16[2,2,256,256]{3,2,1,0:T(8,128)(2,1)} %gather_fusion.7, bf16[2,2,256,256]{3,2,1,0:T(8,128)(2,1)S(1)} %copy-done.15, bf16[2,2,256,256]{3,2,1,0:T(8,128)(2,1)S(1)} %copy-done.16, bf16[2,2,256,256]{3,2,1,0:T(8,128)(2,1)} %gather_fusion.4, ...), kind=kOutput, calls=%fused_computation.15 | convolution fusion | flops 273154048 | bytes 4456460 | tf_op jit(solution)/shard_map/xcil,ml->xcim/dot_general | solution.py:102
  80.8 2.4 %gather_fusion.11 = bf16[2,2,256,256]{3,2,1,0:T(8,128)(2,1)} fusion(bf16[2,2,256,256]{3,2,1,0:T(8,128)(2,1)} %collective-permute-done.5, s32[1024]{0:T(1024)S(1)} %pad_clamp_fusion), kind=kCustom, calls=%fused_computation.11.clone | custom fusion | bytes 1048584 | tf_op jit(solution)/shard_map/jit(_take)/gather | solution.py:95
  83.2 2.4 %gather_fusion.8 = bf16[2,2,256,256]{3,2,1,0:T(8,128)(2,1)} fusion(bf16[2,2,256,256]{3,2,1,0:T(8,128)(2,1)} %collective-permute-done.4, s32[1024]{0:T(1024)S(1)} %pad_clamp_fusion.1), kind=kCustom, calls=%fused_computation.8.clone | custom fusion | bytes 1048584 | tf_op jit(solution)/shard_map/jit(_take)/gather | solution.py:95
  86.7 2.8 %fusion.1 = f32[2,2,256,256]{3,2,1,0:T(8,128)S(1)} fusion(f32[2,2,256,256]{3,2,1,0:T(8,128)} %convolution_add_fusion.1, bf16[2,2,256,256]{3,2,1,0:T(8,128)(2,1)} %gather_fusion.11, bf16[2,2,256,256]{3,2,1,0:T(8,128)(2,1)S(1)} %gather_fusion.10, bf16[2,2,256,256]{3,2,1,0:T(8,128)(2,1)} %gather_fusion.9, bf16[2,2,256,256]{3,2,1,0:T(8,128)(2,1)} %gather_fusion.8, ...), kind=kOutput, calls=%fused_computation.14 | convolution fusion | flops 273940480 | bytes 5505548 | tf_op jit(solution)/shard_map/xcil,ml->xcim/dot_general | solution.py:102
  91.3 2.0 %scatter-add.21 = f32[2,2,256,256]{3,2,1,0:T(8,128)S(1)} dynamic-update-slice(f32[2,2,256,256]{3,2,1,0:T(8,128)S(1)} %scatter-add.20, f32[2,2,64,64]{3,2,1,0:T(8,128)S(1)} %fusion.16, s32[]{:T(128)} %constant.300.clone.1, s32[]{:T(128)} %constant.300.clone.1, s32[]{:T(128)} %constant.305.clone.1, s32[]{:T(128)} %constant.305.clone.1) | dynamic-update-slice | bytes 131076 | tf_op jit(solution)/shard_map/scatter-add | solution.py:136
  96.3 2.7 %collective-permute-start.9 = (f32[2,2,64,64]{3,2,1,0:T(8,128)S(1)}, f32[2,2,64,64]{3,2,1,0:T(8,128)S(1)}, u32[]{:S(2)}, u32[]{:S(2)}) collective-permute-start(f32[2,2,64,64]{3,2,1,0:T(8,128)S(1)} %get-tuple-element.121), channel_id=1, source_target_pairs={{0,1},{1,2},{2,3},{3,4},{4,5},{5,6},{6,7},{7,8},{8,9},{9,10},{10,1... | collective-permute-start | bytes 196616 | tf_op jit(solution)/shard_map/ppermute | solution.py:22
  100.0 6.3 %collective-permute-start.10 = (f32[2,2,64,64]{3,2,1,0:T(8,128)}, f32[2,2,64,64]{3,2,1,0:T(8,128)}, u32[]{:S(2)}, u32[]{:S(2)}) collective-permute-start(f32[2,2,64,64]{3,2,1,0:T(8,128)} %get-tuple-element.120), channel_id=1, source_target_pairs={{1,0},{2,1},{3,2},{4,3},{5,4},{6,5},{7,6},{8,7},{9,8},{10,9},{11,1... | collective-permute-start | bytes 196616 | tf_op jit(solution)/shard_map/ppermute | solution.py:22
  107.5 3.3 %scatter-add.24 = f32[2,2,256,256]{3,2,1,0:T(8,128)} dynamic-update-slice(f32[2,2,256,256]{3,2,1,0:T(8,128)} %copy.31, f32[2,2,64,64]{3,2,1,0:T(8,128)} %fusion.15, s32[]{:T(128)} %constant.300.clone.1, s32[]{:T(128)} %constant.300.clone.1, s32[]{:T(128)} %constant.300.clone.1, s32[]{:T(128)} %constant.300.clone.1) | dynamic-update-slice | bytes 131076 | tf_op jit(solution)/shard_map/scatter-add | solution.py:135
  112.0 1.8 %fusion.14 = f32[2,2,64,64]{3,2,1,0:T(8,128)} fusion(f32[2,2,64,64]{3,2,1,0:T(8,128)S(1)} %convolution_bitcast_fusion.2, f32[2,2,256,256]{3,2,1,0:T(8,128)} %scatter-add.24, f32[1,64,64]{2,1,0:T(8,128)S(1)} %copy-done.12), kind=kOutput, calls=%fused_computation.44 | convolution fusion | flops 12615680 | bytes 212992 | tf_op jit(solution)/shard_map/xcad,ed->xcae/dot_general | solution.py:134
  113.8 3.1 %scatter-add.25 = f32[2,2,256,256]{3,2,1,0:T(8,128)} dynamic-update-slice(f32[2,2,256,256]{3,2,1,0:T(8,128)} %scatter-add.24, f32[2,2,64,64]{3,2,1,0:T(8,128)} %fusion.14, s32[]{:T(128)} %constant.300.clone.1, s32[]{:T(128)} %constant.300.clone.1, s32[]{:T(128)} %constant.305.clone.1, s32[]{:T(128)} %constant.305.clone.1) | dynamic-update-slice | bytes 131076 | tf_op jit(solution)/shard_map/scatter-add | solution.py:136
  117.0 1.8 %fusion.93 = f32[2,256,256]{2,1,0:T(8,128)S(1)} fusion(f32[2,2,256,256]{3,2,1,0:T(8,128)} %scatter-add.25, f32[2,2,256,256]{3,2,1,0:T(8,128)S(1)} %fusion.21), kind=kOutput, calls=%fused_computation.128 | convolution fusion | flops 402653184 | bytes 1572864 | tf_op jit(solution)/shard_map/xij,xjk->xik/dot_general | solution.py:34
  125.1 3.7 %collective-permute-start.11 = (f32[2,2,64,64]{3,2,1,0:T(8,128)S(1)}, f32[2,2,64,64]{3,2,1,0:T(8,128)S(1)}, u32[]{:S(2)}, u32[]{:S(2)}) collective-permute-start(f32[2,2,64,64]{3,2,1,0:T(8,128)S(1)} %get-tuple-element.119), channel_id=1, source_target_pairs={{0,1},{1,2},{2,3},{3,4},{4,5},{5,6},{6,7},{7,8},{8,9},{9,10},{10,1... | collective-permute-start | bytes 196616 | tf_op jit(solution)/shard_map/ppermute | solution.py:22
  129.9 5.3 %collective-permute-start.12 = (f32[2,2,64,64]{3,2,1,0:T(8,128)}, f32[2,2,64,64]{3,2,1,0:T(8,128)S(1)}, u32[]{:S(2)}, u32[]{:S(2)}) collective-permute-start(f32[2,2,64,64]{3,2,1,0:T(8,128)} %get-tuple-element.118), channel_id=1, source_target_pairs={{1,0},{2,1},{3,2},{4,3},{5,4},{6,5},{7,6},{8,7},{9,8},{10,9},{11,1... | collective-permute-start | bytes 196616 | tf_op jit(solution)/shard_map/ppermute | solution.py:22
  139.3 2.0 %scatter-add.29 = f32[2,2,256,256]{3,2,1,0:T(8,128)S(1)} dynamic-update-slice(f32[2,2,256,256]{3,2,1,0:T(8,128)S(1)} %scatter-add.26, f32[2,2,64,64]{3,2,1,0:T(8,128)S(1)} %fusion.12, s32[]{:T(128)} %constant.300.clone.1, s32[]{:T(128)} %constant.300.clone.1, s32[]{:T(128)} %constant.305.clone.1, s32[]{:T(128)} %constant.305.clone.1) | dynamic-update-slice | bytes 131076 | tf_op jit(solution)/shard_map/scatter-add | solution.py:136
  (156 shorter events, 56.9 us)
Async XLA Ops:
  0.0 44.7 %collective-permute-start.1 = (bf16[2,2,256,256]{3,2,1,0:T(8,128)(2,1)}, bf16[2,2,256,256]{3,2,1,0:T(8,128)(2,1)S(1)}, u32[]{:S(2)}, u32[]{:S(2)}) collective-permute-start(bf16[2,2,256,256]{3,2,1,0:T(8,128)(2,1)} %bitcast.226), channel_id=1, source_target_pairs={{0,496},{16,0},{32,16},{48,32},{64,48},{80,64},{96,80},{112,96},{1... | collective-permute-start | bytes 1572872 | tf_op jit(solution)/shard_map/ppermute | solution.py:28
  11.4 38.2 %collective-permute-start = (bf16[2,2,256,256]{3,2,1,0:T(8,128)(2,1)}, bf16[2,2,256,256]{3,2,1,0:T(8,128)(2,1)S(1)}, u32[]{:S(2)}, u32[]{:S(2)}) collective-permute-start(bf16[2,2,256,256]{3,2,1,0:T(8,128)(2,1)} %bitcast.227), channel_id=1, source_target_pairs={{0,16},{16,32},{32,48},{48,64},{64,80},{80,96},{96,112},{112,128},... | collective-permute-start | bytes 1572872 | tf_op jit(solution)/shard_map/ppermute | solution.py:28
  14.9 5.2 %copy-start.12 = (f32[1,64,64]{2,1,0:T(8,128)S(1)}, f32[1,64,64]{2,1,0:T(8,128)}, u32[]{:S(2)}) copy-start(f32[1,64,64]{2,1,0:T(8,128)} %param.32) | copy-start | bytes 49156
  15.6 37.8 %collective-permute-start.6 = (f32[2,2,64,64]{3,2,1,0:T(8,128)}, f32[2,2,64,64]{3,2,1,0:T(8,128)}, u32[]{:S(2)}, u32[]{:S(2)}) collective-permute-start(f32[2,2,64,64]{3,2,1,0:T(8,128)} %get-tuple-element.123), channel_id=1, source_target_pairs={{0,1},{1,2},{2,3},{3,4},{4,5},{5,6},{6,7},{7,8},{8,9},{9,10},{10,1... | collective-permute-start | bytes 196616 | tf_op jit(solution)/shard_map/ppermute | solution.py:22
  20.1 33.3 %collective-permute-start.7 = (f32[1,64,64]{2,1,0:T(8,128)S(1)}, f32[1,64,64]{2,1,0:T(8,128)S(1)}, u32[]{:S(2)}, u32[]{:S(2)}) collective-permute-start(f32[1,64,64]{2,1,0:T(8,128)S(1)} %copy-done.12), channel_id=1, source_target_pairs={{0,1},{1,2},{2,3},{3,4},{4,5},{5,6},{6,7},{7,8},{8,9},{9,10},{10,1... | collective-permute-start | bytes 49160 | tf_op jit(solution)/shard_map/ppermute | solution.py:22
  24.9 27.3 %collective-permute-start.8 = (f32[2,2,64,64]{3,2,1,0:T(8,128)}, f32[2,2,64,64]{3,2,1,0:T(8,128)}, u32[]{:S(2)}, u32[]{:S(2)}) collective-permute-start(f32[2,2,64,64]{3,2,1,0:T(8,128)} %get-tuple-element.122), channel_id=1, source_target_pairs={{1,0},{2,1},{3,2},{4,3},{5,4},{6,5},{7,6},{8,7},{9,8},{10,9},{11,1... | collective-permute-start | bytes 196616 | tf_op jit(solution)/shard_map/ppermute | solution.py:22
  40.0 1.0 copy-start.11
  44.7 12.6 %collective-permute-start.3 = (bf16[2,2,256,256]{3,2,1,0:T(8,128)(2,1)S(1)}, bf16[2,2,256,256]{3,2,1,0:T(8,128)(2,1)S(1)}, u32[]{:S(2)}, u32[]{:S(2)}) collective-permute-start(bf16[2,2,256,256]{3,2,1,0:T(8,128)(2,1)S(1)} %collective-permute-done.1), channel_id=1, source_target_pairs={{0,496},{16,0},{32,16},{48,32},{64,48},{80,64},{96,80},{112,96},{1... | collective-permute-start | bytes 1572872 | tf_op jit(solution)/shard_map/ppermute | solution.py:28
  49.6 13.4 %collective-permute-start.2 = (bf16[2,2,256,256]{3,2,1,0:T(8,128)(2,1)S(1)}, bf16[2,2,256,256]{3,2,1,0:T(8,128)(2,1)S(1)}, u32[]{:S(2)}, u32[]{:S(2)}) collective-permute-start(bf16[2,2,256,256]{3,2,1,0:T(8,128)(2,1)S(1)} %collective-permute-done), channel_id=1, source_target_pairs={{0,16},{16,32},{32,48},{48,64},{64,80},{80,96},{96,112},{112,128},... | collective-permute-start | bytes 1572872 | tf_op jit(solution)/shard_map/ppermute | solution.py:28
  57.3 23.5 %collective-permute-start.5 = (bf16[2,2,256,256]{3,2,1,0:T(8,128)(2,1)S(1)}, bf16[2,2,256,256]{3,2,1,0:T(8,128)(2,1)}, u32[]{:S(2)}, u32[]{:S(2)}) collective-permute-start(bf16[2,2,256,256]{3,2,1,0:T(8,128)(2,1)S(1)} %collective-permute-done.3), channel_id=1, source_target_pairs={{0,496},{16,0},{32,16},{48,32},{64,48},{80,64},{96,80},{112,96},{1... | collective-permute-start | bytes 1572872 | tf_op jit(solution)/shard_map/ppermute | solution.py:28
  63.1 20.1 %collective-permute-start.4 = (bf16[2,2,256,256]{3,2,1,0:T(8,128)(2,1)S(1)}, bf16[2,2,256,256]{3,2,1,0:T(8,128)(2,1)}, u32[]{:S(2)}, u32[]{:S(2)}) collective-permute-start(bf16[2,2,256,256]{3,2,1,0:T(8,128)(2,1)S(1)} %collective-permute-done.2), channel_id=1, source_target_pairs={{0,16},{16,32},{32,48},{48,64},{64,80},{80,96},{96,112},{112,128},... | collective-permute-start | bytes 1572872 | tf_op jit(solution)/shard_map/ppermute | solution.py:28
  75.2 1.4 copy-start.15
  75.2 1.4 copy-start.16
  85.6 1.0 copy-start.24
  96.3 10.0 %collective-permute-start.9 = (f32[2,2,64,64]{3,2,1,0:T(8,128)S(1)}, f32[2,2,64,64]{3,2,1,0:T(8,128)S(1)}, u32[]{:S(2)}, u32[]{:S(2)}) collective-permute-start(f32[2,2,64,64]{3,2,1,0:T(8,128)S(1)} %get-tuple-element.121), channel_id=1, source_target_pairs={{0,1},{1,2},{2,3},{3,4},{4,5},{5,6},{6,7},{7,8},{8,9},{9,10},{10,1... | collective-permute-start | bytes 196616 | tf_op jit(solution)/shard_map/ppermute | solution.py:22
  100.0 10.8 %collective-permute-start.10 = (f32[2,2,64,64]{3,2,1,0:T(8,128)}, f32[2,2,64,64]{3,2,1,0:T(8,128)}, u32[]{:S(2)}, u32[]{:S(2)}) collective-permute-start(f32[2,2,64,64]{3,2,1,0:T(8,128)} %get-tuple-element.120), channel_id=1, source_target_pairs={{1,0},{2,1},{3,2},{4,3},{5,4},{6,5},{7,6},{8,7},{9,8},{10,9},{11,1... | collective-permute-start | bytes 196616 | tf_op jit(solution)/shard_map/ppermute | solution.py:22
  117.0 1.8 %copy-start = (f32[2,2,256,256]{3,2,1,0:T(8,128)S(1)}, f32[2,2,256,256]{3,2,1,0:T(8,128)}, u32[]{:S(2)}) copy-start(f32[2,2,256,256]{3,2,1,0:T(8,128)} %scatter-add.25) | copy-start | bytes 3145732
  122.9 1.2 copy-start.6
  122.9 1.4 copy-start.8
  125.1 11.3 %collective-permute-start.11 = (f32[2,2,64,64]{3,2,1,0:T(8,128)S(1)}, f32[2,2,64,64]{3,2,1,0:T(8,128)S(1)}, u32[]{:S(2)}, u32[]{:S(2)}) collective-permute-start(f32[2,2,64,64]{3,2,1,0:T(8,128)S(1)} %get-tuple-element.119), channel_id=1, source_target_pairs={{0,1},{1,2},{2,3},{3,4},{4,5},{5,6},{6,7},{7,8},{8,9},{9,10},{10,1... | collective-permute-start | bytes 196616 | tf_op jit(solution)/shard_map/ppermute | solution.py:22
  129.9 8.9 %collective-permute-start.12 = (f32[2,2,64,64]{3,2,1,0:T(8,128)}, f32[2,2,64,64]{3,2,1,0:T(8,128)S(1)}, u32[]{:S(2)}, u32[]{:S(2)}) collective-permute-start(f32[2,2,64,64]{3,2,1,0:T(8,128)} %get-tuple-element.118), channel_id=1, source_target_pairs={{1,0},{2,1},{3,2},{4,3},{5,4},{6,5},{7,6},{8,7},{9,8},{10,9},{11,1... | collective-permute-start | bytes 196616 | tf_op jit(solution)/shard_map/ppermute | solution.py:22
  146.1 1.2 copy-start.4
  146.1 1.3 copy-start.9
  146.1 1.5 %copy-start.10 = (f32[2,1,1,256,256]{4,3,0,2,1:T(8,128)S(1)}, f32[2,1,1,256,256]{4,3,0,2,1:T(8,128)}, u32[]{:S(2)}) copy-start(f32[2,1,1,256,256]{4,3,0,2,1:T(8,128)} %get-tuple-element.115) | copy-start | bytes 1572868
  (14 other events, 11.2 us)
where the time goes:
time: 152 us; the launch traced here: 149 us
  starting transfers between devices  59.2 us (39%)
  local copies, waits for them, and re-layouts  41 us (27%)
  matrix products  29.7 us (20%)
  other arithmetic  13.1 us (9%)
  between operations  4.05 us (3%)
  waiting for transfers between devices  1.76 us (1%)
    ppermute x7, starting transfers between devices, from_behind(): lax.ppermute(value, axis, [(source, source + steps) for source in range(f...  31.4 us
    ppermute x6, starting transfers between devices, from_behind_2(): return lax.ppermute(value, axis, pairs)  27.8 us
    gather x12, local copies, waits for them, and re-layouts, on_device(): picked = jnp.take(nearby[place], within, axis=0).astype(jnp.float32)  16.9 us
    dot_general x3, matrix products, on_device(): jnp.einsum('xcil,ml->xcim', half, matrix, preferred_element_type=jnp.floa...  9.82 us
    unnamed x52, local copies, waits for them, and re-layouts  7.89 us
    scatter-add x3, local copies, waits for them, and re-layouts, on_device(): system = system.at[:, :, orbitals - face:, orbitals - face:].add(-outer)  7.21 us
    scatter-add x3, local copies, waits for them, and re-layouts, on_device(): system = base.at[:, :, :face, :face].add(-inner)  5.7 us
    and x6, other arithmetic, on_device(): picked = jnp.take(nearby[place], within, axis=0).astype(jnp.float32)  4.23 us
  transfers between devices with their start and end apart: 13, of which 2 were waited for; matrix products, arithmetic and copies ran while one was open for 29% of the time, Pallas kernels for 0%

commit v1 on v0

v1 whole, which is shorter than its diff:
```python
import jax
import jax.numpy as jnp
from jax import lax
from jax.experimental import pallas as pl
from jax.experimental.pallas import tpu as pltpu
from jax.sharding import PartitionSpec as P

MAXCELL = 8

broadening = 0.05
contact_width = 0.15
damping = 0.75
level_start = -0.05
level_range = 0.1

B = 256
F = 64
F32 = jnp.float32
BF16 = jnp.bfloat16
VMEM = pl.BlockSpec(memory_space=pltpu.VMEM)
SMEM = pl.BlockSpec(memory_space=pltpu.SMEM)
highest = lax.Precision.HIGHEST


def mm(left, right):
    return jnp.dot(left, right, preferred_element_type=F32)


def mm_nt(left, right):
    return lax.dot_general(left, right, (((1,), (1,)), ((), ())), preferred_element_type=F32)


def exact(left, right):
    return jnp.dot(left, right, precision=highest, preferred_element_type=F32)


def halves(value):
    high = value.astype(BF16)
    return high, (value - high.astype(F32)).astype(BF16)


def mm3(left, right):
    return mm(left[0], right[0]) + (mm(left[0], right[1]) + mm(left[1], right[0]))


def complex_mm(left, right):
    real = mm3(left[0], right[0]) - mm3(left[1], right[1])
    imag = mm3(left[0], right[1]) + mm3(left[1], right[0])
    return real, imag


def levels():
    first = lax.axis_index("energy") * 2
    energies = 2 * lax.axis_size("energy")
    return [level_start + level_range * (first + e).astype(F32) / energies for e in range(2)]


def inverse(real, width):
    denom = real * real + width * width
    return real / denom, -width / denom


def call(kernel, outs, n_smem, n_vmem, flops, scratch=(), **kw):
    return pl.pallas_call(
        kernel,
        out_shape=[jax.ShapeDtypeStruct(shape, dtype) for shape, dtype in outs],
        in_specs=[SMEM] * n_smem + [VMEM] * n_vmem,
        out_specs=[VMEM] * len(outs),
        scratch_shapes=list(scratch),
        cost_estimate=pl.CostEstimate(flops=flops, bytes_accessed=1 << 20, transcendentals=0),
        compiler_params=pltpu.CompilerParams(vmem_limit_bytes=32 << 20),
        **kw,
    )


def pack_kernel(contact, interface, offset, out):
    out[...] = jnp.zeros_like(out)
    out[0:F, 0:F] = interface[...]
    out[F : F + 1, :] = offset[:, 0:128]
    out[F + 1 : F + 2, :] = offset[:, 128:256]
    out[F + 2 : F + 3, :] = jnp.full((1, 128), contact[0].astype(F32))


def pick(odd, when_even, when_odd):
    return jnp.where(odd, when_odd, when_even)


def prepare_kernel(hopping, own, recv_e, recv_o, base, packed0, self0, rows, cols, mats):
    slab = lax.axis_index("slab")
    odd = slab % 2 == 1
    before = pick(odd, recv_o[...], recv_e[...])
    after = pick(odd, recv_e[...], recv_o[...])
    mine = own[...]
    has_after = jnp.where(slab < lax.axis_size("slab") - 1, 1.0, 0.0)
    level = levels()
    zero = jnp.zeros((F, 128), F32)

    def width_of(pack):
        return broadening + contact_width * pack[F + 2 : F + 3, :]

    def column(row):
        return jnp.broadcast_to(row, (128, 128)).T

    def down(matrix):
        return jnp.concatenate((matrix, zero), 0)

    def up(matrix):
        return jnp.concatenate((zero, matrix), 0)

    v_own, v_before = mine[0:F], before[0:F]
    mats[0] = up(v_own).T.astype(BF16)
    mats[1] = up(v_own).astype(BF16)
    mats[2] = down(v_before).astype(BF16)
    mats[3] = down(v_before).T.astype(BF16)

    def inner_of(pack, e):
        v = pack[0:F]
        w = width_of(pack)[:, 0:1]
        real, imag = inverse(level[e] + column(pack[F + 1 : F + 2])[F:128], w)
        return [exact(down(v * x).T, down(v))[0:F] for x in (real, imag)]

    def outer_of(v, pack, e):
        real, imag = inverse(level[e] + pack[F : F + 1], width_of(pack))
        return [exact(v * x, down(v).T) for x in (real, imag)]

    sym = hopping[...].astype(F32)
    sym = 0.5 * (sym + sym.T)
    left_row, right_row = mine[F : F + 1], mine[F + 1 : F + 2]
    left_col, right_col = column(left_row), column(right_row)
    width = width_of(mine)
    for e in range(2):
        inner = inner_of(before, e)
        outer = [x * has_after for x in outer_of(v_own, after, e)]
        to_right = inner_of(mine, e)
        to_left = outer_of(v_before, mine, e)
        base[e, 0] = sym
        base[e, 1] = jnp.zeros((B, B), F32)
        for c in range(2):
            base[e, c, 0:F, 0:128] += inner[c]
            base[e, c, B - F : B, 128:256] += pltpu.roll(outer[c], F, 1)
        packed0[e, 0] = inner[0] + pltpu.roll(inner[1], F, 1)
        packed0[e, 1] = outer[0] + pltpu.roll(outer[1], F, 1)
        self0[e, 0] = to_right[0] + pltpu.roll(to_right[1], F, 1)
        self0[e, 1] = to_left[0] + pltpu.roll(to_left[1], F, 1)
        for part, (row, col) in enumerate(((left_row, left_col), (right_row, right_col))):
            lanes = slice(128 * part, 128 * part + 128)
            real, imag = inverse(level[e] + row, width)
            rows[2 * e : 2 * e + 1, lanes] = real
            rows[2 * e + 1 : 2 * e + 2, lanes] = imag
            real, imag = inverse(level[e] + col, width[:, 0:1])
            cols[3 * e, lanes] = real
            cols[3 * e + 1, lanes] = imag
            cols[3 * e + 2, lanes] = level[e] + col
    rows[4:8, :] = jnp.broadcast_to(width[:, 0:1], (4, B))


def write_pair(pair, slot, shift, mode, direct, swapped, direct_low, swapped_low):
    second = lax.axis_index("energy") % 2 == 1
    is_odd = shift == 2 * mode + 1

    def put(e, first, other):
        for c in range(2):
            pair[slot, e, c] = (first[c].astype(F32) + other[c].astype(F32)).astype(BF16)

    @pl.when(jnp.logical_not(is_odd))
    def _():
        for e in range(2):
            put(e, direct.at[e], swapped.at[e])

    if direct_low is not None:

        @pl.when(jnp.logical_and(is_odd, jnp.logical_not(second)))
        def _():
            put(0, direct.at[1], swapped_low.at[1])
            put(1, direct_low.at[0], swapped.at[0])

        @pl.when(jnp.logical_and(is_odd, second))
        def _():
            put(0, swapped.at[1], direct_low.at[1])
            put(1, swapped_low.at[0], direct.at[0])


def sigma_low_kernel(shift, cells, own, d1, w1, d2, w2, coupling, base, out, pair):
    write_pair(pair, 0, shift[0], 0, d1, w1, own, own)
    write_pair(pair, 1, shift[1], 1, d2, w2, d1, w1)
    weight = cells[0].astype(F32) / MAXCELL
    for e in range(2):
        for c in range(2):
            total = None
            for k in range(2):
                half = mm(coupling[k], pair[k, e, c]).astype(BF16)
                term = mm_nt(half, coupling[k])
                total = term if total is None else total + term
            out[e, c] = base[e, c] + weight * total


def send_faces(e, w_real, w_imag, mats, self0, send_e, send_o, odd):
    right = [mm(mm(mats[0, 0:F], w[128:256, 128:256]).astype(BF16), mats[1]) for w in (w_real, w_imag)]
    left = [mm(mm(mats[2, 0:F], w[0:128, 0:128]).astype(BF16), mats[3]) for w in (w_real, w_imag)]
    to_right = right[0] + pltpu.roll(right[1], F, 1) + self0[e, 0]
    to_left = left[0] + pltpu.roll(left[1], F, 1) + self0[e, 1]
    send_e[e] = pick(odd, to_right, to_left).astype(BF16)
    send_o[e] = pick(odd, to_left, to_right).astype(BF16)


def twice(column):
    return jnp.concatenate((column, column), 1)


def first_kernel(cells, d3, w3, coupling, low, rows, cols, mats, self0, n0, w1, send_e, send_o):
    odd = lax.axis_index("slab") % 2 == 1
    weight = cells[0].astype(F32) / MAXCELL
    for e in range(2):
        n = []
        for c in range(2):
            pair = (d3[e, c].astype(F32) + w3[e, c].astype(F32)).astype(BF16)
            half = mm(coupling[2], pair).astype(BF16)
            value = low[e, c] + weight * mm_nt(half, coupling[2])
            n0[e, c] = value
            n.append(value)
        xr, xi = rows[2 * e : 2 * e + 1], rows[2 * e + 1 : 2 * e + 2]
        tr = damping * (n[0] * xr - n[1] * xi)
        ti = damping * (n[0] * xi + n[1] * xr)
        cr, ci = twice(cols[3 * e]), twice(cols[3 * e + 1])
        wr = cr * tr - ci * ti
        wi = cr * ti + ci * tr
        w1[e, 0] = wr
        w1[e, 1] = wi
        send_faces(e, wr.astype(BF16), wi.astype(BF16), mats, self0, send_e, send_o, odd)


def step_kernel(last, n0, w, rows, cols, out):
    for e in range(2):
        xr, xi = rows[2 * e : 2 * e + 1], rows[2 * e + 1 : 2 * e + 2]
        cr, ci = twice(cols[3 * e]), twice(cols[3 * e + 1])
        nr, ni, wr, wi = n0[e, 0], n0[e, 1], w[e, 0], w[e, 1]
        pr = nr * xr - ni * xi
        pi = nr * xi + ni * xr
        n_split = (halves(nr), halves(ni))
        w_split = (halves(wr), halves(wi))
        rr, ri = complex_mm(n_split, w_split)
        if last:
            dr, di = twice(cols[3 * e + 2]), rows[4:5]
            rr = rr + (pr - (dr * wr - di * wi))
            ri = ri + (pi - (dr * wi + di * wr))
        else:
            rr = rr + 0.25 * pr
            ri = ri + 0.25 * pi
        yr, yi = complex_mm(w_split, (halves(rr), halves(ri)))
        out[e, 0] = wr + damping * (cr * rr - ci * ri + yr)
        out[e, 1] = wi + damping * (cr * ri + ci * rr + yi)


def face_rows(part, w, rows, e):
    at = slice(0, F) if part == 0 else slice(B - F, B)
    index = lax.broadcasted_iota(jnp.int32, (F, B), 0) + (0 if part == 0 else B - F)
    here = lax.broadcasted_iota(jnp.int32, (F, B), 1) == index
    real = w[e, 0, at] + jnp.where(here, rows[2 * e : 2 * e + 1], 0.0)
    imag = w[e, 1, at] + jnp.where(here, rows[2 * e + 1 : 2 * e + 2], 0.0)
    return real, imag


def add_faces(e, recv, packed0, w, done, rows, cols, change):
    scaled = []
    for part, at in ((0, slice(0, F)), (1, slice(B - F, B))):
        delta = (recv[part].astype(F32) - packed0[e, part]).astype(BF16)
        real, imag = face_rows(part, w, rows, e)
        rr = mm(delta, jnp.concatenate((real, -imag), 0).astype(BF16))
        ri = mm(delta, jnp.concatenate((imag, real), 0).astype(BF16))
        change[0, at] = rr.astype(BF16)
        change[1, at] = ri.astype(BF16)
        cr, ci = twice(cols[3 * e, at]), twice(cols[3 * e + 1, at])
        scaled.append((damping * (cr * rr - ci * ri), damping * (cr * ri + ci * rr)))
    wr, wi = w[e, 0].astype(BF16), w[e, 1].astype(BF16)
    qr, qi = change[0], change[1]
    yr = done[e, 0] + damping * (mm(wr, qr) - mm(wi, qi))
    yi = done[e, 1] + damping * (mm(wr, qi) + mm(wi, qr))
    zero = jnp.zeros((B - 2 * F, B), F32)
    yr = yr + jnp.concatenate((scaled[0][0], zero, scaled[1][0]), 0)
    yi = yi + jnp.concatenate((scaled[0][1], zero, scaled[1][1]), 0)
    return yr, yi


def clear(change):
    change[...] = jnp.zeros_like(change)


def second_kernel(recv_e, recv_o, packed0, w1, done, rows, cols, mats, self0, w2, send_e, send_o, change):
    odd = lax.axis_index("slab") % 2 == 1
    clear(change)
    for e in range(2):
        inner = pick(odd, recv_o[e], recv_e[e])
        outer = pick(odd, recv_e[e], recv_o[e])
        yr, yi = add_faces(e, (inner, outer), packed0, w1, done, rows, cols, change.at[e])
        w2[e, 0] = yr
        w2[e, 1] = yi
        send_faces(e, yr.astype(BF16), yi.astype(BF16), mats, self0, send_e, send_o, odd)


def third_kernel(recv_e, recv_o, packed0, w2, done, rows, cols, out, change):
    odd = lax.axis_index("slab") % 2 == 1
    clear(change)
    for e in range(2):
        inner = pick(odd, recv_o[e], recv_e[e])
        outer = pick(odd, recv_e[e], recv_o[e])
        yr, yi = add_faces(e, (inner, outer), packed0, w2, done, rows, cols, change.at[e])
        index = lax.broadcasted_iota(jnp.int32, (B, B), 0)
        here = lax.broadcasted_iota(jnp.int32, (B, B), 1) == index
        out[e, 0] = yr + jnp.where(here, rows[2 * e : 2 * e + 1], 0.0)
        out[e, 1] = yi + jnp.where(here, rows[2 * e + 1 : 2 * e + 2], 0.0)


def on_device(
    green_old,
    hopping,
    phonon_coupling,
    band_offset,
    interface,
    cell_counts,
    contact_flags,
    phonon_shift,
):
    stops = lax.axis_size("energy")
    slabs = lax.axis_size("slab")
    outer_pairs = [(e, (e + 1) % stops) if e % 2 == 1 else (e, (e - 1) % stops) for e in range(stops)]
    same_core = [(e, (e + 2) % stops) if e % 2 == 0 else (e, (e - 2) % stops) for e in range(stops)]
    partner = [(e, e ^ 1) for e in range(stops)]
    even_pairs = [(s, s ^ 1) for s in range(slabs)]
    odd_pairs = [(s, ((s + 1) ^ 1) - 1) for s in range(1, slabs - 1)]

    def move(value, pairs):
        return lax.ppermute(value, "energy", pairs)

    def exchange(to_even, to_odd):
        return lax.ppermute(to_even, "slab", even_pairs), lax.ppermute(to_odd, "slab", odd_pairs)

    own = green_old[:, 0]
    coupling = phonon_coupling[0]
    full = ((2, 2, B, B), F32)
    faces = ((2, F, 128), BF16)
    packs = ((2, 2, F, 128), F32)

    d1 = move(own, outer_pairs)
    w1 = move(own, partner)
    (pack,) = call(pack_kernel, [((72, 128), F32)], 1, 2, 1 << 10)(
        contact_flags, interface[0], band_offset
    )
    near, pack, _ = lax.optimization_barrier((own, pack, w1))
    d2 = move(near, same_core)
    pack_e, pack_o = exchange(pack, pack)
    d3 = move(d1, same_core)
    w2 = move(d1, partner)
    w3 = move(d2, partner)
    base, packed0, self0, rows, cols, mats = call(
        prepare_kernel,
        [full, packs, packs, ((8, B), F32), ((6, B, 128), F32), ((4, 128, 128), BF16)],
        0,
        4,
        1 << 20,
    )(hopping[0], pack, pack_e, pack_o)
    (low,) = call(
        sigma_low_kernel,
        [full],
        2,
        7,
        32 << 24,
        scratch=[pltpu.VMEM((2, 2, 2, B, B), BF16)],
    )(phonon_shift, cell_counts, own, d1, w1, d2, w2, coupling, base)
    n0, x1, send_e, send_o = call(first_kernel, [full, full, faces, faces], 1, 8, 16 << 24)(
        cell_counts, d3, w3, coupling, low, rows, cols, mats, self0
    )
    recv_e, recv_o = exchange(send_e, send_o)
    (done,) = call(lambda *refs: step_kernel(False, *refs), [full], 0, 4, 96 << 24)(n0, x1, rows, cols)
    change = [pltpu.VMEM((2, 2, B, B), BF16)]
    x2, send_e, send_o = call(second_kernel, [full, faces, faces], 0, 9, 16 << 24, scratch=change)(
        recv_e, recv_o, packed0, x1, done, rows, cols, mats, self0
    )
    recv_e, recv_o = exchange(send_e, send_o)
    (done,) = call(lambda *refs: step_kernel(True, *refs), [full], 0, 4, 96 << 24)(n0, x2, rows, cols)
    (out,) = call(third_kernel, [full], 0, 7, 16 << 24, scratch=change)(
        recv_e, recv_o, packed0, x2, done, rows, cols
    )
    return out[:, None]


def solution(mesh):
    placed = (
        P("energy", "slab", None, None, None),
        P("slab", None, None),
        P("slab", None, None, None),
        P("slab", None),
        P("slab", None, None),
        P("slab"),
        P("slab"),
        P(),
    )
    return jax.shard_map(
        on_device,
        mesh=mesh,
        in_specs=placed,
        out_specs=P("energy", "slab", None, None, None),
        check_vma=False,
    )
```

time: 152 us -> 82.6 us (0.54); the launches traced: 149 us -> 81.9 us
  local copies, waits for them, and re-layouts: 41 us -> 5.02 us
  matrix products: 29.7 us -> 0 us
  other arithmetic: 13.1 us -> 0 us
  Pallas kernels: 0 us -> 12.8 us
  waiting for transfers between devices: 1.76 us -> 13.8 us
  starting transfers between devices: 59.2 us -> 48.8 us
  between operations: 4.05 us -> 1.52 us
    dot_general x31 -> x0, matrix products: 29.7 us -> none  [the longest x3 9.82 us: on_device(): jnp.einsum('xcil,ml->xcim', half, matrix, preferred_element_type=jnp.floa...]
    gather x12 -> x0, local copies, waits for them, and re-layouts: 16.9 us -> none  [on_device(): picked = jnp.take(nearby[place], within, axis=0).astype(jnp.float32)]
    scatter-add x6 -> x0, local copies, waits for them, and re-layouts: 12.9 us -> none  [the longest x3 7.21 us: on_device(): system = system.at[:, :, orbitals - face:, orbitals - face:].add(-outer)]
    pallas_call x0 -> x8, Pallas kernels: none -> 12.8 us  [the longest x1 2.39 us: on_device(): call(lambda *refs: step_kernel(True, *refs), [full], 0, 4, 96 << 24)]
    ppermute x13 -> x12, waiting for transfers between devices: 1.76 us -> 13.8 us  [the longest x6 7.65 us: move(): return lax.ppermute(value, 'energy', pairs)]
    ppermute x13 -> x12, starting transfers between devices: 59.2 us -> 48.8 us  [the longest x6 23.2 us: move(): return lax.ppermute(value, 'energy', pairs)]
    and x6 -> x0, other arithmetic: 4.23 us -> none  [on_device(): picked = jnp.take(nearby[place], within, axis=0).astype(jnp.float32)]
    unnamed x52 -> x14, local copies, waits for them, and re-layouts: 7.89 us -> 5.02 us
  transfers between devices with their start and end apart: 13 -> 12, of which waited for: 2 -> 5; matrix products, arithmetic and copies ran while one was open for 29% -> 0% of each run, Pallas kernels for 0% -> 9%
where the time goes in v1:
time: 82.6 us; the launch traced here: 81.9 us
  starting transfers between devices  48.8 us (59%)
  waiting for transfers between devices  13.8 us (17%)
  Pallas kernels  12.8 us (15%)
  local copies, waits for them, and re-layouts  5.02 us (6%)
  between operations  1.52 us (2%)
    ppermute x6, starting transfers between devices, move(): return lax.ppermute(value, 'energy', pairs)  23.2 us
    ppermute x3, starting transfers between devices, exchange(): lax.ppermute(to_odd, 'slab', odd_pairs)  15 us
    ppermute x3, starting transfers between devices, exchange(): lax.ppermute(to_even, 'slab', even_pairs)  10.7 us
    ppermute x6, waiting for transfers between devices, move(): return lax.ppermute(value, 'energy', pairs)  7.65 us
    ppermute x3, waiting for transfers between devices, exchange(): lax.ppermute(to_odd, 'slab', odd_pairs)  6.15 us
    unnamed x14, local copies, waits for them, and re-layouts  5.02 us
    pallas_call x1, Pallas kernels, on_device(): call(lambda *refs: step_kernel(True, *refs), [full], 0, 4, 96 << 24)  2.39 us
    pallas_call x1, Pallas kernels, on_device(): call(lambda *refs: step_kernel(False, *refs), [full], 0, 4, 96 << 24)  2.26 us
  transfers between devices with their start and end apart: 12, of which 5 were waited for; matrix products, arithmetic and copies ran while one was open for 0% of the time, Pallas kernels for 9%

profile of v1, /device:TPU:6, one launch (start us, length us, event | category | flops | bytes accessed | tf_op | source)
XLA Modules:
  0.0 81.9 jit_solution(13602838781359712683)
XLA Ops:
  0.0 1.9 %collective-permute-start.2 = (bf16[2,2,256,256]{3,2,1,0:T(8,128)(2,1)}, bf16[2,2,256,256]{3,2,1,0:T(8,128)(2,1)S(1)}, u32[]{:S(2)}, u32[]{:S(2)}) collective-permute-start(bf16[2,2,256,256]{3,2,1,0:T(8,128)(2,1)} %bitcast.9), channel_id=1, source_target_pairs={{0,16},{16,0},{32,48},{48,32},{64,80},{80,64},{96,112},{112,96},{1... | collective-permute-start | bytes 1572872 | tf_op jit(solution)/shard_map/ppermute | solution.py:332
  1.9 12.1 %collective-permute-start = (bf16[2,2,256,256]{3,2,1,0:T(8,128)(2,1)}, bf16[2,2,256,256]{3,2,1,0:T(8,128)(2,1)S(1)}, u32[]{:S(2)}, u32[]{:S(2)}) collective-permute-start(bf16[2,2,256,256]{3,2,1,0:T(8,128)(2,1)} %bitcast.10), channel_id=1, source_target_pairs={{0,496},{16,32},{32,16},{48,64},{64,48},{80,96},{96,80},{112,128},... | collective-permute-start | bytes 1572872 | tf_op jit(solution)/shard_map/ppermute | solution.py:332
  16.1 1.9 %collective-permute-start.3 = (bf16[2,2,256,256]{3,2,1,0:T(8,128)(2,1)}, bf16[2,2,256,256]{3,2,1,0:T(8,128)(2,1)S(1)}, u32[]{:S(2)}, u32[]{:S(2)}) collective-permute-start(bf16[2,2,256,256]{3,2,1,0:T(8,128)(2,1)} %bitcast.11), channel_id=1, source_target_pairs={{0,32},{16,496},{32,64},{48,16},{64,96},{80,48},{96,128},{112,80},... | collective-permute-start | bytes 1572872 | tf_op jit(solution)/shard_map/ppermute | solution.py:332
  18.0 5.1 %collective-permute-done.d1 = bf16[2,2,256,256]{3,2,1,0:T(8,128)(2,1)S(1)} collective-permute-done((bf16[2,2,256,256]{3,2,1,0:T(8,128)(2,1)}, bf16[2,2,256,256]{3,2,1,0:T(8,128)(2,1)S(1)}, u32[]{:S(2)}, u32[]{:S(2)}) %collective-permute-start) | collective-permute-done | bytes 524320 | tf_op jit(solution)/shard_map/ppermute | solution.py:332
  23.1 1.9 %collective-permute-start.5 = (bf16[2,2,256,256]{3,2,1,0:T(8,128)(2,1)S(1)}, bf16[2,2,256,256]{3,2,1,0:T(8,128)(2,1)S(1)}, u32[]{:S(2)}, u32[]{:S(2)}) collective-permute-start(bf16[2,2,256,256]{3,2,1,0:T(8,128)(2,1)S(1)} %collective-permute-done.d1), channel_id=1, source_target_pairs={{0,16},{16,0},{32,48},{48,32},{64,80},{80,64},{96,112},{112,96},{1... | collective-permute-start | bytes 1572872 | tf_op jit(solution)/shard_map/ppermute | solution.py:332
  25.1 1.9 %collective-permute-start.1 = (bf16[2,2,256,256]{3,2,1,0:T(8,128)(2,1)S(1)}, bf16[2,2,256,256]{3,2,1,0:T(8,128)(2,1)S(1)}, u32[]{:S(2)}, u32[]{:S(2)}) collective-permute-start(bf16[2,2,256,256]{3,2,1,0:T(8,128)(2,1)S(1)} %collective-permute-done.d1), channel_id=1, source_target_pairs={{0,32},{16,496},{32,64},{48,16},{64,96},{80,48},{96,128},{112,80},... | collective-permute-start | bytes 1572872 | tf_op jit(solution)/shard_map/ppermute | solution.py:332
  27.0 2.5 %collective-permute-done.3.d2 = bf16[2,2,256,256]{3,2,1,0:T(8,128)(2,1)S(1)} collective-permute-done((bf16[2,2,256,256]{3,2,1,0:T(8,128)(2,1)}, bf16[2,2,256,256]{3,2,1,0:T(8,128)(2,1)S(1)}, u32[]{:S(2)}, u32[]{:S(2)}) %collective-permute-start.3) | collective-permute-done | bytes 524320 | tf_op jit(solution)/shard_map/ppermute | solution.py:332
  29.5 3.4 %collective-permute-start.4 = (bf16[2,2,256,256]{3,2,1,0:T(8,128)(2,1)S(1)}, bf16[2,2,256,256]{3,2,1,0:T(8,128)(2,1)S(1)}, u32[]{:S(2)}, u32[]{:S(2)}) collective-permute-start(bf16[2,2,256,256]{3,2,1,0:T(8,128)(2,1)S(1)} %collective-permute-done.3.d2), channel_id=1, source_target_pairs={{0,16},{16,0},{32,48},{48,32},{64,80},{80,64},{96,112},{112,96},{1... | collective-permute-start | bytes 1572872 | tf_op jit(solution)/shard_map/ppermute | solution.py:332
  32.9 4.5 %collective-permute-start.6 = (f32[72,128]{1,0:T(8,128)S(1)}, f32[72,128]{1,0:T(8,128)S(1)}, u32[]{:S(2)}, u32[]{:S(2)}) collective-permute-start(f32[72,128]{1,0:T(8,128)S(1)} %shard_map.82.own), channel_id=1, source_target_pairs={{0,1},{1,0},{2,3},{3,2},{4,5},{5,4},{6,7},{7,6},{8,9},{9,8},{10,11... | collective-permute-start | bytes 110600 | tf_op jit(solution)/shard_map/ppermute | solution.py:335
  37.4 5.1 %collective-permute-start.7 = (f32[72,128]{1,0:T(8,128)S(1)}, f32[72,128]{1,0:T(8,128)S(1)}, u32[]{:S(2)}, u32[]{:S(2)}) collective-permute-start(f32[72,128]{1,0:T(8,128)S(1)} %shard_map.82.own), channel_id=1, source_target_pairs={{1,2},{2,1},{3,4},{4,3},{5,6},{6,5},{7,8},{8,7},{9,10},{10,9},{11,... | collective-permute-start | bytes 110600 | tf_op jit(solution)/shard_map/ppermute | solution.py:335
  43.2 3.1 %collective-permute-done.7.recv_o = f32[72,128]{1,0:T(8,128)S(1)} collective-permute-done((f32[72,128]{1,0:T(8,128)S(1)}, f32[72,128]{1,0:T(8,128)S(1)}, u32[]{:S(2)}, u32[]{:S(2)}) %collective-permute-start.7) | collective-permute-done | bytes 36896 | tf_op jit(solution)/shard_map/ppermute | solution.py:335
  47.2 1.2 %shard_map.83 = (f32[2,2,256,256]{3,2,1,0:T(8,128)S(1)}, f32[2,2,64,128]{3,2,1,0:T(8,128)S(1)}, f32[2,2,64,128]{3,2,1,0:T(8,128)S(1)}, f32[8,256]{1,0:T(8,128)S(...) custom-call(bf16[256,256]{1,0:T(8,128)(2,1)S(1)} %bitcast.13, f32[72,128]{1,0:T(8,128)S(1)} %shard_map.82.own, ...), custom_call_target="tpu_custom_call" | custom-call | flops 1048576 | bytes 1048576 | tf_op jit(solution)/shard_map/pallas_call | solution.py:354
  51.1 1.8 %shard_map.84.low = f32[2,2,256,256]{3,2,1,0:T(8,128)S(1)} custom-call(s32[3]{0:T(128)S(1)} %copy-done.6, s32[1]{0:T(128)S(6)} %copy.10.cells, bf16[2,2,256,256]{3,2,1,0:T(8,128)(2,1)S(1)} %bitcast.12, bf16[2,2,256,256]{3,2,1,0:T(8,128)(2,1)S(1)} %collective-permute-done.d1, bf16[2,2,256,256]{3,2,1,0:T(8,128)(2,1)S(1)} %collective-permute-done.2.w1, ...), custom_call_target="tpu_custom_call" | custom-call | flops 536870912 | bytes 1048576 | tf_op jit(solution)/shard_map/pallas_call | solution.py:361
  52.9 1.7 %shard_map.85 = (f32[2,2,256,256]{3,2,1,0:T(8,128)S(1)}, f32[2,2,256,256]{3,2,1,0:T(8,128)S(1)}, bf16[2,64,128]{2,1,0:T(8,128)(2,1)S(1)}, bf16[2,64,128]{2,1,0:T(8,128)(2,1)S(1)}) custom-call(s32[1]{0:T(128)S(6)} %copy.10.cells, bf16[2,2,256,256]{3,2,1,0:T(8,128)(2,1)S(1)} %collective-permute-done.1.d3, ...), custom_call_target="tpu_custom_call" | custom-call | flops 268435456 | bytes 1048576 | tf_op jit(solution)/shard_map/pallas_call | solution.py:369
  54.6 1.9 %collective-permute-start.8 = (bf16[2,64,128]{2,1,0:T(8,128)(2,1)S(1)}, bf16[2,64,128]{2,1,0:T(8,128)(2,1)S(1)}, u32[]{:S(2)}, u32[]{:S(2)}) collective-permute-start(bf16[2,64,128]{2,1,0:T(8,128)(2,1)S(1)} %get-tuple-element.27), channel_id=1, source_target_pairs={{0,1},{1,0},{2,3},{3,2},{4,5},{5,4},{6,7},{7,6},{8,9},{9,8},{10,11... | collective-permute-start | bytes 98312 | tf_op jit(solution)/shard_map/ppermute | solution.py:335
  56.5 5.1 %collective-permute-start.9 = (bf16[2,64,128]{2,1,0:T(8,128)(2,1)S(1)}, bf16[2,64,128]{2,1,0:T(8,128)(2,1)S(1)}, u32[]{:S(2)}, u32[]{:S(2)}) collective-permute-start(bf16[2,64,128]{2,1,0:T(8,128)(2,1)S(1)} %get-tuple-element.28), channel_id=1, source_target_pairs={{1,2},{2,1},{3,4},{4,3},{5,6},{6,5},{7,8},{8,7},{9,10},{10,9},{11,... | collective-permute-start | bytes 98312 | tf_op jit(solution)/shard_map/ppermute | solution.py:335
  61.6 2.3 %shard_map.86.done = f32[2,2,256,256]{3,2,1,0:T(8,128)S(1)} custom-call(f32[2,2,256,256]{3,2,1,0:T(8,128)S(1)} %get-tuple-element.31.refs_0_, f32[2,2,256,256]{3,2,1,0:T(8,128)S(1)} %get-tuple-element.30.refs_1_.w1, f32[8,256]{1,0:T(8,128)S(1)} %get-tuple-element.23.rows.refs_2_, f32[6,256,128]{2,1,0:T(8,128)S(1)} %get-tuple-element.24.cols.refs_3_), custom_call_target="tpu_custom_call" | custom-call | flops 1610612736 | bytes 1048576 | tf_op jit(solution)/shard_map/pallas_call | solution.py:373
  63.9 1.5 %collective-permute-done.9.recv_o = bf16[2,64,128]{2,1,0:T(8,128)(2,1)S(1)} collective-permute-done((bf16[2,64,128]{2,1,0:T(8,128)(2,1)S(1)}, bf16[2,64,128]{2,1,0:T(8,128)(2,1)S(1)}, u32[]{:S(2)}, u32[]{:S(2)}) %collective-permute-start.9) | collective-permute-done | bytes 32800 | tf_op jit(solution)/shard_map/ppermute | solution.py:335
  65.4 1.7 %shard_map.87 = (f32[2,2,256,256]{3,2,1,0:T(8,128)S(1)}, bf16[2,64,128]{2,1,0:T(8,128)(2,1)S(1)}, bf16[2,64,128]{2,1,0:T(8,128)(2,1)S(1)}) custom-call(bf16[2,64,128]{2,1,0:T(8,128)(2,1)S(1)} %collective-permute-done.8.recv_e, bf16[2,64,128]{2,1,0:T(8,128)(2,1)S(1)} %collective-permute-done.9.recv_o, f32[2,2,64,128]{3,2,1,0:T(8,128)S(1)} %get-tuple-element.29.packed0, ...), custom_call_target="tpu_custom_call" | custom-call | flops 268435456 | bytes 1048576 | tf_op jit(solution)/shard_map/pallas_call | solution.py:375
  67.1 4.3 %collective-permute-start.10 = (bf16[2,64,128]{2,1,0:T(8,128)(2,1)S(1)}, bf16[2,64,128]{2,1,0:T(8,128)(2,1)S(1)}, u32[]{:S(2)}, u32[]{:S(2)}) collective-permute-start(bf16[2,64,128]{2,1,0:T(8,128)(2,1)S(1)} %get-tuple-element.32), channel_id=1, source_target_pairs={{0,1},{1,0},{2,3},{3,2},{4,5},{5,4},{6,7},{7,6},{8,9},{9,8},{10,11... | collective-permute-start | bytes 98312 | tf_op jit(solution)/shard_map/ppermute | solution.py:335
  71.4 4.8 %collective-permute-start.11 = (bf16[2,64,128]{2,1,0:T(8,128)(2,1)S(1)}, bf16[2,64,128]{2,1,0:T(8,128)(2,1)S(1)}, u32[]{:S(2)}, u32[]{:S(2)}) collective-permute-start(bf16[2,64,128]{2,1,0:T(8,128)(2,1)S(1)} %get-tuple-element.33), channel_id=1, source_target_pairs={{1,2},{2,1},{3,4},{4,3},{5,6},{6,5},{7,8},{8,7},{9,10},{10,9},{11,... | collective-permute-start | bytes 98312 | tf_op jit(solution)/shard_map/ppermute | solution.py:335
  76.2 2.4 %shard_map.88.done = f32[2,2,256,256]{3,2,1,0:T(8,128)S(1)} custom-call(f32[2,2,256,256]{3,2,1,0:T(8,128)S(1)} %get-tuple-element.31.refs_0_, f32[2,2,256,256]{3,2,1,0:T(8,128)S(1)} %get-tuple-element.34.refs_1_.w2, f32[8,256]{1,0:T(8,128)S(1)} %get-tuple-element.23.rows.refs_2_, f32[6,256,128]{2,1,0:T(8,128)S(1)} %get-tuple-element.24.cols.refs_3_), custom_call_target="tpu_custom_call" | custom-call | flops 1610612736 | bytes 1048576 | tf_op jit(solution)/shard_map/pallas_call | solution.py:379
  78.6 1.6 %collective-permute-done.11.recv_o = bf16[2,64,128]{2,1,0:T(8,128)(2,1)S(1)} collective-permute-done((bf16[2,64,128]{2,1,0:T(8,128)(2,1)S(1)}, bf16[2,64,128]{2,1,0:T(8,128)(2,1)S(1)}, u32[]{:S(2)}, u32[]{:S(2)}) %collective-permute-start.11) | collective-permute-done | bytes 32800 | tf_op jit(solution)/shard_map/ppermute | solution.py:335
  80.2 1.8 %shard_map.89 = f32[2,2,256,256]{3,2,1,0:T(8,128)} custom-call(bf16[2,64,128]{2,1,0:T(8,128)(2,1)S(1)} %collective-permute-done.10.recv_e, bf16[2,64,128]{2,1,0:T(8,128)(2,1)S(1)} %collective-permute-done.11.recv_o, f32[2,2,64,128]{3,2,1,0:T(8,128)S(1)} %get-tuple-element.29.packed0, f32[2,2,256,256]{3,2,1,0:T(8,128)S(1)} %get-tuple-element.34.refs_1_.w2, ...), custom_call_target="tpu_custom_call" | custom-call | flops 268435456 | bytes 1048576 | tf_op jit(solution)/shard_map/pallas_call | solution.py:380
  (22 shorter events, 5.1 us)
Async XLA Ops:
  0.0 16.1 %collective-permute-start.2 = (bf16[2,2,256,256]{3,2,1,0:T(8,128)(2,1)}, bf16[2,2,256,256]{3,2,1,0:T(8,128)(2,1)S(1)}, u32[]{:S(2)}, u32[]{:S(2)}) collective-permute-start(bf16[2,2,256,256]{3,2,1,0:T(8,128)(2,1)} %bitcast.9), channel_id=1, source_target_pairs={{0,16},{16,0},{32,48},{48,32},{64,80},{80,64},{96,112},{112,96},{1... | collective-permute-start | bytes 1572872 | tf_op jit(solution)/shard_map/ppermute | solution.py:332
  1.9 21.2 %collective-permute-start = (bf16[2,2,256,256]{3,2,1,0:T(8,128)(2,1)}, bf16[2,2,256,256]{3,2,1,0:T(8,128)(2,1)S(1)}, u32[]{:S(2)}, u32[]{:S(2)}) collective-permute-start(bf16[2,2,256,256]{3,2,1,0:T(8,128)(2,1)} %bitcast.10), channel_id=1, source_target_pairs={{0,496},{16,32},{32,16},{48,64},{64,48},{80,96},{96,80},{112,128},... | collective-permute-start | bytes 1572872 | tf_op jit(solution)/shard_map/ppermute | solution.py:332
  14.6 0.7 copy-start.5
  15.3 0.8 copy-start.4
  16.1 13.4 %collective-permute-start.3 = (bf16[2,2,256,256]{3,2,1,0:T(8,128)(2,1)}, bf16[2,2,256,256]{3,2,1,0:T(8,128)(2,1)S(1)}, u32[]{:S(2)}, u32[]{:S(2)}) collective-permute-start(bf16[2,2,256,256]{3,2,1,0:T(8,128)(2,1)} %bitcast.11), channel_id=1, source_target_pairs={{0,32},{16,496},{32,64},{48,16},{64,96},{80,48},{96,128},{112,80},... | collective-permute-start | bytes 1572872 | tf_op jit(solution)/shard_map/ppermute | solution.py:332
  23.1 25.3 %collective-permute-start.5 = (bf16[2,2,256,256]{3,2,1,0:T(8,128)(2,1)S(1)}, bf16[2,2,256,256]{3,2,1,0:T(8,128)(2,1)S(1)}, u32[]{:S(2)}, u32[]{:S(2)}) collective-permute-start(bf16[2,2,256,256]{3,2,1,0:T(8,128)(2,1)S(1)} %collective-permute-done.d1), channel_id=1, source_target_pairs={{0,16},{16,0},{32,48},{48,32},{64,80},{80,64},{96,112},{112,96},{1... | collective-permute-start | bytes 1572872 | tf_op jit(solution)/shard_map/ppermute | solution.py:332
  25.1 27.9 %collective-permute-start.1 = (bf16[2,2,256,256]{3,2,1,0:T(8,128)(2,1)S(1)}, bf16[2,2,256,256]{3,2,1,0:T(8,128)(2,1)S(1)}, u32[]{:S(2)}, u32[]{:S(2)}) collective-permute-start(bf16[2,2,256,256]{3,2,1,0:T(8,128)(2,1)S(1)} %collective-permute-done.d1), channel_id=1, source_target_pairs={{0,32},{16,496},{32,64},{48,16},{64,96},{80,48},{96,128},{112,80},... | collective-permute-start | bytes 1572872 | tf_op jit(solution)/shard_map/ppermute | solution.py:332
  29.5 23.4 %collective-permute-start.4 = (bf16[2,2,256,256]{3,2,1,0:T(8,128)(2,1)S(1)}, bf16[2,2,256,256]{3,2,1,0:T(8,128)(2,1)S(1)}, u32[]{:S(2)}, u32[]{:S(2)}) collective-permute-start(bf16[2,2,256,256]{3,2,1,0:T(8,128)(2,1)S(1)} %collective-permute-done.3.d2), channel_id=1, source_target_pairs={{0,16},{16,0},{32,48},{48,32},{64,80},{80,64},{96,112},{112,96},{1... | collective-permute-start | bytes 1572872 | tf_op jit(solution)/shard_map/ppermute | solution.py:332
  32.9 10.2 %collective-permute-start.6 = (f32[72,128]{1,0:T(8,128)S(1)}, f32[72,128]{1,0:T(8,128)S(1)}, u32[]{:S(2)}, u32[]{:S(2)}) collective-permute-start(f32[72,128]{1,0:T(8,128)S(1)} %shard_map.82.own), channel_id=1, source_target_pairs={{0,1},{1,0},{2,3},{3,2},{4,5},{5,4},{6,7},{7,6},{8,9},{9,8},{10,11... | collective-permute-start | bytes 110600 | tf_op jit(solution)/shard_map/ppermute | solution.py:335
  37.4 8.9 %collective-permute-start.7 = (f32[72,128]{1,0:T(8,128)S(1)}, f32[72,128]{1,0:T(8,128)S(1)}, u32[]{:S(2)}, u32[]{:S(2)}) collective-permute-start(f32[72,128]{1,0:T(8,128)S(1)} %shard_map.82.own), channel_id=1, source_target_pairs={{1,2},{2,1},{3,4},{4,3},{5,6},{6,5},{7,8},{8,7},{9,10},{10,9},{11,... | collective-permute-start | bytes 110600 | tf_op jit(solution)/shard_map/ppermute | solution.py:335
  46.3 0.9 %copy-start.3 = (bf16[1,256,256]{2,1,0:T(8,128)(2,1)S(1)}, bf16[1,256,256]{2,1,0:T(8,128)(2,1)}, u32[]{:S(2)}) copy-start(bf16[1,256,256]{2,1,0:T(8,128)(2,1)} %param.9) | copy-start | bytes 393220
  48.4 0.7 copy-start.6
  49.1 1.0 %copy-start = (bf16[1,3,256,256]{3,2,1,0:T(8,128)(2,1)S(1)}, bf16[1,3,256,256]{3,2,1,0:T(8,128)(2,1)}, u32[]{:S(2)}) copy-start(bf16[1,3,256,256]{3,2,1,0:T(8,128)(2,1)} %param.10) | copy-start | bytes 1179652
  50.1 1.0 %copy-start.2 = (bf16[2,1,2,256,256]{4,3,2,1,0:T(8,128)(2,1)S(1)}, bf16[2,1,2,256,256]{4,3,2,1,0:T(8,128)(2,1)}, u32[]{:S(2)}) copy-start(bf16[2,1,2,256,256]{4,3,2,1,0:T(8,128)(2,1)} %param.8) | copy-start | bytes 1572868
  51.1 1.8 %copy-start.1 = (bf16[1,3,256,256]{3,2,1,0:T(8,128)(2,1)S(1)}, bf16[1,3,256,256]{3,2,1,0:T(8,128)(2,1)}, u32[]{:S(2)}) copy-start(bf16[1,3,256,256]{3,2,1,0:T(8,128)(2,1)} %param.10) | copy-start | bytes 1179652
  54.6 9.3 %collective-permute-start.8 = (bf16[2,64,128]{2,1,0:T(8,128)(2,1)S(1)}, bf16[2,64,128]{2,1,0:T(8,128)(2,1)S(1)}, u32[]{:S(2)}, u32[]{:S(2)}) collective-permute-start(bf16[2,64,128]{2,1,0:T(8,128)(2,1)S(1)} %get-tuple-element.27), channel_id=1, source_target_pairs={{0,1},{1,0},{2,3},{3,2},{4,5},{5,4},{6,7},{7,6},{8,9},{9,8},{10,11... | collective-permute-start | bytes 98312 | tf_op jit(solution)/shard_map/ppermute | solution.py:335
  56.5 8.8 %collective-permute-start.9 = (bf16[2,64,128]{2,1,0:T(8,128)(2,1)S(1)}, bf16[2,64,128]{2,1,0:T(8,128)(2,1)S(1)}, u32[]{:S(2)}, u32[]{:S(2)}) collective-permute-start(bf16[2,64,128]{2,1,0:T(8,128)(2,1)S(1)} %get-tuple-element.28), channel_id=1, source_target_pairs={{1,2},{2,1},{3,4},{4,3},{5,6},{6,5},{7,8},{8,7},{9,10},{10,9},{11,... | collective-permute-start | bytes 98312 | tf_op jit(solution)/shard_map/ppermute | solution.py:335
  67.1 11.5 %collective-permute-start.10 = (bf16[2,64,128]{2,1,0:T(8,128)(2,1)S(1)}, bf16[2,64,128]{2,1,0:T(8,128)(2,1)S(1)}, u32[]{:S(2)}, u32[]{:S(2)}) collective-permute-start(bf16[2,64,128]{2,1,0:T(8,128)(2,1)S(1)} %get-tuple-element.32), channel_id=1, source_target_pairs={{0,1},{1,0},{2,3},{3,2},{4,5},{5,4},{6,7},{7,6},{8,9},{9,8},{10,11... | collective-permute-start | bytes 98312 | tf_op jit(solution)/shard_map/ppermute | solution.py:335
  71.4 8.8 %collective-permute-start.11 = (bf16[2,64,128]{2,1,0:T(8,128)(2,1)S(1)}, bf16[2,64,128]{2,1,0:T(8,128)(2,1)S(1)}, u32[]{:S(2)}, u32[]{:S(2)}) collective-permute-start(bf16[2,64,128]{2,1,0:T(8,128)(2,1)S(1)} %get-tuple-element.33), channel_id=1, source_target_pairs={{1,2},{2,1},{3,4},{4,3},{5,6},{6,5},{7,8},{8,7},{9,10},{10,9},{11,... | collective-permute-start | bytes 98312 | tf_op jit(solution)/shard_map/ppermute | solution.py:335
